TPU v7x, 32 devices: a whole 2x2x4 slice. The times are simulated.
32 devices in a mesh: cuts: 4 (over z), blk: 2 (over x), rep: 4 (over y, core).
Axes of the slice: x: 2, y: 2, z: 4, core: 2. Of those that a mesh axis runs over, the one named last changes fastest.
Arguments:
- features: bfloat16 [8192, 256], P(('cuts', 'blk', 'rep')), may hold values from -6 to 6
- adj_values: bfloat16 [64, 4, 128, 1024], P(('cuts', 'blk'), 'rep'), as said below
- adj_cols: int32 [64, 4, 8], P(('cuts', 'blk'), 'rep'), may hold values from 0 to 15, as said below
- adj_count: int32 [64, 4], P(('cuts', 'blk'), 'rep'), may hold values from 1 to 8, as said below
- weight: bfloat16 [256, 256], replicated, may hold values from -0.375 to 0.375
- cotangent: bfloat16 [8192, 256], P(('cuts', 'blk', 'rep')), may hold values from -6 to 6
Outputs:
- output: bfloat16 [8192, 256], P(('cuts', 'blk', 'rep'))
- weight_grad: float32 [256, 256], replicated
Inputs may be any that keep to these rules, and one draw needn't show every extreme that they name: `adj_values`: entries are nonnegative; a row of a block has about 8 nonzero entries on average. `adj_cols`: within one row block and rep index the 8 numbers are distinct. `adj_count`: in every aligned group of 8 row blocks, for every rep index, some row block has count 8.
All inputs are finite; a program needn't handle non-finite values.
Results may differ from a plain program's by a relative error of at most 0.0061.
Values may be sent and summed in bfloat16 or wider, within the bound.
A program may use at most 64 MiB of HBM per device.

v0:
```python
import jax
import jax.numpy as jnp
from jax import lax
from jax.sharding import PartitionSpec as P


def silu_grad(pre):
    sigmoid_z = jax.nn.sigmoid(pre)
    return sigmoid_z * (1.0 + pre * (1.0 - sigmoid_z))


def local(features, adj_values, adj_cols, adj_count, weight, cotangent):
    block_size = adj_values.shape[2]
    slot_count = adj_cols.shape[2]
    feature_width = features.shape[1]
    group_rows = adj_values.shape[0]
    in_slice = lax.all_gather(features, "blk", axis=0, tiled=True)
    gathered = lax.all_gather(in_slice, "cuts", axis=0, tiled=True)
    panel_blocks = gathered.reshape(-1, block_size, feature_width)
    columns = adj_cols[:, 0, :]
    picked = panel_blocks[columns]
    slot_ids = jnp.arange(slot_count, dtype=jnp.int32)[None, :]
    usable = slot_ids < adj_count[:, 0][:, None]
    picked = jnp.where(usable[:, :, None, None], picked, jnp.zeros((), jnp.bfloat16))
    picked = picked.reshape(group_rows, slot_count * block_size, feature_width)
    partial_value = lax.dot_general(
        adj_values[:, 0], picked, (((2,), (1,)), ((0,), (0,))), preferred_element_type=jnp.float32
    )
    partial_value = partial_value.reshape(group_rows * block_size, feature_width)
    summed = lax.psum_scatter(partial_value, "rep", scatter_dimension=0, tiled=True)
    hidden = summed.astype(jnp.bfloat16)
    pre = jnp.dot(hidden, weight, preferred_element_type=jnp.float32)
    output = jax.nn.silu(pre).astype(jnp.bfloat16)
    grad_pre = (cotangent.astype(jnp.float32) * silu_grad(pre)).astype(jnp.bfloat16)
    local_grad = lax.dot_general(
        hidden, grad_pre, (((0,), (0,)), ((), ())), preferred_element_type=jnp.float32
    )
    weight_grad = lax.psum(local_grad, ("cuts", "blk", "rep"))
    return (output, weight_grad)


def solution(mesh):
    placed = (
        P(("cuts", "blk", "rep"), None),
        P(("cuts", "blk"), "rep", None, None),
        P(("cuts", "blk"), "rep", None),
        P(("cuts", "blk"), "rep"),
        P(),
        P(("cuts", "blk", "rep"), None),
    )
    return jax.shard_map(
        local,
        mesh=mesh,
        in_specs=placed,
        out_specs=(P(("cuts", "blk", "rep"), None), P()),
        check_vma=False,
    )
```

profile of v0, /device:TPU:0, one launch (start us, length us, event | category | flops | bytes accessed | tf_op | source)
XLA Modules:
  0.0 220.4 jit_solution(18052649329132863206)
XLA Ops:
  7.2 0.0 copy-start
  7.2 0.0 all-gather.2.cloned.1.call-start
  7.2 9.1 %all_gather.6 = bf16[512,256]{1,0:T(8,128)(2,1)} all-gather(bf16[256,256]{1,0:T(8,128)(2,1)} %param.6), channel_id=1, replica_groups=mesh['cuts'=4,'blk'=2,'rep'=4] {'blk'}, dimensions={0}, use_global_device_ids=true | all-gather | bytes 393216 | tf_op jit(solution)/shard_map/all_gather | solution.py:17
  16.4 0.0 all-gather.2.cloned.1.call-update
  16.4 0.0 reduce-scatter.2.cloned.1.call-start
  16.4 0.7 compare_select_fusion
  17.1 0.1 reshape.67
  17.2 0.7 iota_compare_fusion
  17.9 0.1 broadcast_bitcast_fusion
  18.0 26.9 %all-gather.2.cloned.1.call-done = bf16[2048,256]{1,0:T(8,128)(2,1)} async-done(((bf16[512,256]{1,0:T(8,128)(2,1)}), bf16[2048,256]{1,0:T(8,128)(2,1)}) %all-gather.2.cloned.1.call-update) | async-done | bytes 1048592 | tf_op jit(solution)/shard_map/all_gather | solution.py:18
  44.8 4.0 %gather_fusion = bf16[64,128,256]{2,1,0:T(8,128)(2,1)} fusion(bf16[16,128,256]{2,1,0:T(8,128)(2,1)} %bitcast.19, s32[1024]{0:T(1024)S(1)} %pad_clamp_fusion), kind=kCustom, calls=%fused_computation | custom fusion | bytes 8388864 | tf_op jit(solution)/shard_map/gather | solution.py:21
  48.8 4.6 %bitcast_select_fusion = bf16[8,1024,256]{2,1,0:T(8,128)(2,1)S(1)} fusion(pred[8,1024]{1,0:T(8,128)(4,1)S(1)} %broadcast_bitcast_fusion, bf16[8,1024,256]{2,1,0:T(8,128)(2,1)} %bitcast.18), kind=kLoop, calls=%fused_computation.1 | loop fusion | flops 2097152 | bytes 8396800 | tf_op jit(solution)/shard_map/jit(_where)/select_n | solution.py:24
  53.4 0.0 copy-done
  53.4 0.0 copy-start.1
  53.4 0.0 copy-start.2
  53.4 1.8 fusion
  55.2 0.0 reduce-scatter.2.cloned.1.call-update
  55.2 0.0 all-reduce.2.cloned.1.call-start
  55.3 24.2 %reduce-scatter.2.cloned.1.call-done = f32[256,256]{1,0:T(8,128)} async-done(((f32[1024,256]{1,0:T(8,128)}), f32[256,256]{1,0:T(8,128)}) %reduce-scatter.2.cloned.1.call-update) | async-done | bytes 262160 | tf_op jit(solution)/shard_map/reduce_scatter | solution.py:30
  79.5 0.0 copy-done.1
  79.5 1.8 multiply_convert_fusion.1
  81.4 0.0 copy-done.2
  81.4 1.9 fusion.2
  83.3 0.0 all-reduce.2.cloned.1.call-update
  83.3 128.8 %all-reduce.2.cloned.1.call-done = f32[256,256]{1,0:T(8,128)} async-done(((f32[256,256]{1,0:T(8,128)}), f32[256,256]{1,0:T(8,128)}) %all-reduce.2.cloned.1.call-update) | async-done | bytes 262160 | tf_op jit(solution)/shard_map/psum | solution.py:38
  212.2 1.7 copy.9
  (1 shorter events, 0.0 us)
Async XLA Ops:
  7.2 46.2 %copy-start = (bf16[8,1,128,1024]{3,2,1,0:T(8,128)(2,1)S(1)}, bf16[8,1,128,1024]{3,2,1,0:T(8,128)(2,1)}, u32[]{:S(2)}) copy-start(bf16[8,1,128,1024]{3,2,1,0:T(8,128)(2,1)} %param.7) | copy-start | bytes 6291460
  7.2 37.7 %all-gather.2.cloned.1.call-start = ((), (), s32[]{:S(2)}) async-start(), calls=%async_computation.1 | async-start | bytes 1310720 | tf_op jit(solution)/shard_map/all_gather | solution.py:18
  16.4 63.1 %reduce-scatter.2.cloned.1.call-start = ((), (), s32[]{:S(2)}) async-start(), calls=%async_computation.2 | async-start | bytes 1310720 | tf_op jit(solution)/shard_map/reduce_scatter | solution.py:30
  53.4 26.1 %copy-start.1 = (bf16[256,256]{1,0:T(8,128)(2,1)S(1)}, bf16[256,256]{1,0:T(8,128)(2,1)}, u32[]{:S(2)}) copy-start(bf16[256,256]{1,0:T(8,128)(2,1)} %param.10) | copy-start | bytes 393220
  53.4 27.9 %copy-start.2 = (bf16[256,256]{1,0:T(8,128)(2,1)S(1)}, bf16[256,256]{1,0:T(8,128)(2,1)}, u32[]{:S(2)}) copy-start(bf16[256,256]{1,0:T(8,128)(2,1)} %param.11) | copy-start | bytes 393220
  55.2 157.0 %all-reduce.2.cloned.1.call-start = ((), (), s32[]{:S(2)}) async-start(), calls=%async_computation.3 | async-start | bytes 524288 | tf_op jit(solution)/shard_map/psum | solution.py:38
Sparse Core Ops, SparseCore 0:
  16.5 28.2 all-gather.1
  55.3 24.1 reduce-scatter.1
  85.6 126.5 all-reduce.1
where the time goes:
time: 221 us; the launch traced here: 220 us
  waiting for transfers between devices  180 us (81%)
  between operations  13.8 us (6%)
  blocking collectives  9.13 us (4%)
  other arithmetic  5.95 us (3%)
  local copies, waits for them, and re-layouts  5.83 us (3%)
  matrix products  5.53 us (3%)
    psum x1, waiting for transfers between devices, local(): weight_grad = lax.psum(local_grad, ('cuts', 'blk', 'rep'))  129 us
    all_gather x1, waiting for transfers between devices, local(): gathered = lax.all_gather(in_slice, 'cuts', axis=0, tiled=True)  26.9 us
    reduce_scatter x1, waiting for transfers between devices, local(): lax.psum_scatter(partial_value, 'rep', scatter_dimension=0, tiled=True)  24.2 us
    all_gather x1, blocking collectives, local(): in_slice = lax.all_gather(features, 'blk', axis=0, tiled=True)  9.13 us
    select_n x1, other arithmetic, local(): jnp.where(usable[:, :, None, None], picked, jnp.zeros((), jnp.bfloat16))  4.58 us
  transfers between devices with their start and end apart: 3, of which 3 were waited for; matrix products, arithmetic and copies ran while one was open for 1% of the time, Pallas kernels for 0%

commit v1 on v0

--- a/solution.py
+++ b/solution.py
@@ -2,6 +2,11 @@
 import jax.numpy as jnp
 from jax import lax
 from jax.sharding import PartitionSpec as P
+
+
+def one_after_other(array, first, second):
+    half = lax.psum(array, first)
+    return lax.psum(half, second)
 
 
 def silu_grad(pre):
@@ -35,7 +40,7 @@
     local_grad = lax.dot_general(
         hidden, grad_pre, (((0,), (0,)), ((), ())), preferred_element_type=jnp.float32
     )
-    weight_grad = lax.psum(local_grad, ("cuts", "blk", "rep"))
+    weight_grad = one_after_other(local_grad, "cuts", ("blk", "rep"))
     return (output, weight_grad)
 
 

time: 221 us -> 184 us (0.83)
  waiting for transfers between devices: 180 us -> 144 us
    psum x1 -> x2, waiting for transfers between devices: 129 us -> 92.4 us  [the longest x1 56.7 us: one_after_other(): return lax.psum(half, second)]
  transfers between devices with their start and end apart: 3 -> 4, of which waited for: 3 -> 4; matrix products, arithmetic and copies ran while one was open for 1% -> 1% of each run, Pallas kernels for 0% -> 0%
where the time goes in v1:
time: 184 us
  waiting for transfers between devices  144 us (78%)
  between operations  13.8 us (8%)
  blocking collectives  9.13 us (5%)
  other arithmetic  5.95 us (3%)
  local copies, waits for them, and re-layouts  5.83 us (3%)
  matrix products  5.53 us (3%)
    psum x1, waiting for transfers between devices, one_after_other(): return lax.psum(half, second)  56.7 us
    psum x1, waiting for transfers between devices, one_after_other(): half = lax.psum(array, first)  35.7 us
    all_gather x1, waiting for transfers between devices, local(): gathered = lax.all_gather(in_slice, 'cuts', axis=0, tiled=True)  26.9 us
    reduce_scatter x1, waiting for transfers between devices, local(): lax.psum_scatter(partial_value, 'rep', scatter_dimension=0, tiled=True)  24.2 us
    all_gather x1, blocking collectives, local(): in_slice = lax.all_gather(features, 'blk', axis=0, tiled=True)  9.13 us
    select_n x1, other arithmetic, local(): jnp.where(usable[:, :, None, None], picked, jnp.zeros((), jnp.bfloat16))  4.58 us
    gather x1, local copies, waits for them, and re-layouts, local(): picked = panel_blocks[columns]  3.98 us
  transfers between devices with their start and end apart: 4, of which 4 were waited for; matrix products, arithmetic and copies ran while one was open for 1% of the time, Pallas kernels for 0%

profile of v1, /device:TPU:0, one launch (start us, length us, event | category | flops | bytes accessed | tf_op | source)
XLA Modules:
  0.0 184.0 jit_solution(17050339815561848411)
XLA Ops:
  7.2 0.0 copy-start
  7.2 0.0 all-gather.2.cloned.1.call-start
  7.2 9.1 %all_gather.6 = bf16[512,256]{1,0:T(8,128)(2,1)} all-gather(bf16[256,256]{1,0:T(8,128)(2,1)} %param.6), channel_id=1, replica_groups=mesh['cuts'=4,'blk'=2,'rep'=4] {'blk'}, dimensions={0}, use_global_device_ids=true | all-gather | bytes 393216 | tf_op jit(solution)/shard_map/all_gather | solution.py:22
  16.4 0.0 all-gather.2.cloned.1.call-update
  16.4 0.0 reduce-scatter.2.cloned.1.call-start
  16.4 0.7 compare_select_fusion
  17.1 0.1 reshape.67
  17.2 0.7 iota_compare_fusion
  17.9 0.1 broadcast_bitcast_fusion
  18.0 26.9 %all-gather.2.cloned.1.call-done = bf16[2048,256]{1,0:T(8,128)(2,1)} async-done(((bf16[512,256]{1,0:T(8,128)(2,1)}), bf16[2048,256]{1,0:T(8,128)(2,1)}) %all-gather.2.cloned.1.call-update) | async-done | bytes 1048592 | tf_op jit(solution)/shard_map/all_gather | solution.py:23
  44.8 4.0 %gather_fusion = bf16[64,128,256]{2,1,0:T(8,128)(2,1)} fusion(bf16[16,128,256]{2,1,0:T(8,128)(2,1)} %bitcast.19, s32[1024]{0:T(1024)S(1)} %pad_clamp_fusion), kind=kCustom, calls=%fused_computation | custom fusion | bytes 8388864 | tf_op jit(solution)/shard_map/gather | solution.py:26
  48.8 4.6 %bitcast_select_fusion = bf16[8,1024,256]{2,1,0:T(8,128)(2,1)S(1)} fusion(pred[8,1024]{1,0:T(8,128)(4,1)S(1)} %broadcast_bitcast_fusion, bf16[8,1024,256]{2,1,0:T(8,128)(2,1)} %bitcast.18), kind=kLoop, calls=%fused_computation.1 | loop fusion | flops 2097152 | bytes 8396800 | tf_op jit(solution)/shard_map/jit(_where)/select_n | solution.py:29
  53.4 0.0 copy-done
  53.4 0.0 copy-start.1
  53.4 0.0 copy-start.2
  53.4 1.8 fusion
  55.2 0.0 reduce-scatter.2.cloned.1.call-update
  55.2 0.0 all-reduce.3.cloned.1.call-start
  55.3 24.2 %reduce-scatter.2.cloned.1.call-done = f32[256,256]{1,0:T(8,128)} async-done(((f32[1024,256]{1,0:T(8,128)}), f32[256,256]{1,0:T(8,128)}) %reduce-scatter.2.cloned.1.call-update) | async-done | bytes 262160 | tf_op jit(solution)/shard_map/reduce_scatter | solution.py:35
  79.5 0.0 copy-done.1
  79.5 1.8 multiply_convert_fusion.1
  81.4 0.0 copy-done.2
  81.4 1.9 %fusion.2 = f32[256,256]{1,0:T(8,128)} fusion(f32[256,256]{1,0:T(8,128)S(1)} %get-tuple-element.3, bf16[256,256]{1,0:T(8,128)(2,1)S(1)} %copy-done.2, f32[256,256]{1,0:T(8,128)} %reduce-scatter.2.cloned.1.call-done), kind=kOutput, calls=%fused_computation.7 | convolution fusion | flops 34275328 | bytes 917504 | tf_op jit(solution)/shard_map/dot_general | solution.py:40
  83.3 0.0 all-reduce.3.cloned.1.call-update
  83.3 0.0 all-reduce.5.cloned.1.call-start
  83.4 35.7 %all-reduce.3.cloned.1.call-done = f32[256,256]{1,0:T(8,128)} async-done(((f32[256,256]{1,0:T(8,128)}), f32[256,256]{1,0:T(8,128)}) %all-reduce.3.cloned.1.call-update) | async-done | bytes 262160 | tf_op jit(solution)/shard_map/psum | solution.py:8
  119.1 0.0 all-reduce.5.cloned.1.call-update
  119.1 56.7 %all-reduce.5.cloned.1.call-done = f32[256,256]{1,0:T(8,128)} async-done(((f32[256,256]{1,0:T(8,128)}), f32[256,256]{1,0:T(8,128)}) %all-reduce.5.cloned.1.call-update) | async-done | bytes 262160 | tf_op jit(solution)/shard_map/psum | solution.py:9
  175.8 1.7 copy.10
  (1 shorter events, 0.0 us)
Async XLA Ops:
  7.2 46.2 %copy-start = (bf16[8,1,128,1024]{3,2,1,0:T(8,128)(2,1)S(1)}, bf16[8,1,128,1024]{3,2,1,0:T(8,128)(2,1)}, u32[]{:S(2)}) copy-start(bf16[8,1,128,1024]{3,2,1,0:T(8,128)(2,1)} %param.7) | copy-start | bytes 6291460
  7.2 37.7 %all-gather.2.cloned.1.call-start = ((), (), s32[]{:S(2)}) async-start(), calls=%async_computation.1 | async-start | bytes 1310720 | tf_op jit(solution)/shard_map/all_gather | solution.py:23
  16.4 63.1 %reduce-scatter.2.cloned.1.call-start = ((), (), s32[]{:S(2)}) async-start(), calls=%async_computation.2 | async-start | bytes 1310720 | tf_op jit(solution)/shard_map/reduce_scatter | solution.py:35
  53.4 26.1 %copy-start.1 = (bf16[256,256]{1,0:T(8,128)(2,1)S(1)}, bf16[256,256]{1,0:T(8,128)(2,1)}, u32[]{:S(2)}) copy-start(bf16[256,256]{1,0:T(8,128)(2,1)} %param.10) | copy-start | bytes 393220
  53.4 27.9 %copy-start.2 = (bf16[256,256]{1,0:T(8,128)(2,1)S(1)}, bf16[256,256]{1,0:T(8,128)(2,1)}, u32[]{:S(2)}) copy-start(bf16[256,256]{1,0:T(8,128)(2,1)} %param.11) | copy-start | bytes 393220
  55.2 63.9 %all-reduce.3.cloned.1.call-start = ((), (), s32[]{:S(2)}) async-start(), calls=%async_computation.3 | async-start | bytes 524288 | tf_op jit(solution)/shard_map/psum | solution.py:8
  83.3 92.4 %all-reduce.5.cloned.1.call-start = ((), (), s32[]{:S(2)}) async-start(), calls=%async_computation.4 | async-start | bytes 524288 | tf_op jit(solution)/shard_map/psum | solution.py:9
Sparse Core Ops, SparseCore 0:
  16.5 28.2 all-gather.1
  55.3 24.1 reduce-scatter.1
  83.4 35.5 all-reduce.2
  122.0 53.7 all-reduce.4
